TPU v7x, 32 devices: a whole 2x2x4 slice. The times are simulated.
32 devices in a mesh: row: 8 (over z, core), col: 4 (over y, x).
Axes of the slice: x: 2, y: 2, z: 4, core: 2. Of those that a mesh axis runs over, the one named last changes fastest.
Arguments:
- roll_hidden: bfloat16 [1344, 4096], P(('row', 'col')), may hold values from -6 to 6
- roll_cotangent: bfloat16 [1344, 4096], P(('row', 'col')), may hold values from -6 to 6
- lengths: int32 [32], P(('row', 'col')), may hold values from 1 to 42, as said below
- owners: int32 [32], P(('row', 'col')), may hold values from 0 to 7, as said below
- prompts: int32 [32], P(('row', 'col')), may hold values from 0 to 3
- rewards: float32 [32], P(('row', 'col')), may hold values from -5 to 5
- gate_weight: bfloat16 [4096, 14784], P('col', 'row'), may hold values from -0.09375 to 0.09375
- up_weight: bfloat16 [4096, 14784], P('col', 'row'), may hold values from -0.09375 to 0.09375
- down_weight: bfloat16 [14784, 4096], P('row', 'col'), may hold values from -0.046875 to 0.046875
Outputs:
- grad_input: bfloat16 [1024, 4096], P('row', 'col')
- grad_gate: bfloat16 [4096, 14784], P('col', 'row')
- grad_up: bfloat16 [4096, 14784], P('col', 'row')
- grad_down: bfloat16 [14784, 4096], P('row', 'col')
Inputs may be any that keep to these rules, and one draw needn't show every extreme that they name: `owners`: each owner value names exactly 4 rows; the lengths of one owner's rows sum to at most 128, and to exactly 128 for some owner in every draw. `lengths`: some row has length 42 in every draw.
All inputs are finite; a program needn't handle non-finite values.
Results may differ from a plain program's by a relative error of at most 0.025.
Values may be sent and summed in bfloat16 or wider, within the bound.
A program may use at most 128 MiB of HBM per device.

v0:
```python
import jax
import jax.numpy as jnp
from jax import lax
from jax.sharding import PartitionSpec as P

CAPR = 128
spread_floor = 0.7


def row_weights(lengths, prompts, rewards, count_prompts):
    onehot = (prompts[:, None] == jnp.arange(count_prompts, dtype=jnp.int32)[None, :]).astype(
        jnp.float32
    )
    counts = jnp.maximum(jnp.sum(onehot, 0), 1.0)
    means = jnp.sum(onehot * rewards[:, None], 0) / counts
    centred = rewards - jnp.sum(onehot * means[None, :], 1)
    spreads = jnp.sqrt(jnp.sum(onehot * (centred * centred)[:, None], 0) / counts)
    divisor = jnp.maximum(jnp.sum(onehot * spreads[None, :], 1), spread_floor)
    return centred / divisor / lengths.astype(jnp.float32)


def row_offsets(lengths, owners):
    count = lengths.shape[0]
    places = jnp.arange(count, dtype=jnp.int32)
    earlier = (owners[None, :] == owners[:, None]) & (places[None, :] < places[:, None])
    return jnp.sum(jnp.where(earlier, lengths[None, :], 0), 1)


def source_index(lengths, owners, offsets, slot_count, capacity, total):
    count = lengths.shape[0]
    slots = jnp.arange(slot_count, dtype=jnp.int32)
    live = slots[None, :] < lengths[:, None]
    target = jnp.where(live, owners[:, None] * capacity + offsets[:, None] + slots[None, :], total)
    flat_source = slots[None, :] * count + jnp.arange(count, dtype=jnp.int32)[:, None]
    empty = jnp.full((total,), slot_count * count, jnp.int32)
    return empty.at[target.reshape(-1)].set(flat_source.reshape(-1), mode="drop")


def per_device(
    roll_hidden,
    roll_cotangent,
    lengths,
    owners,
    prompts,
    rewards,
    gate_weight,
    up_weight,
    down_weight,
):
    row_count = lax.axis_size("row")
    col_count = lax.axis_size("col")
    total_tokens = row_count * CAPR
    count_prompts = row_count * col_count // 8
    slot_count = roll_hidden.shape[0]
    width = roll_hidden.shape[1] // col_count
    local = jnp.stack(
        [
            lengths.astype(jnp.float32),
            owners.astype(jnp.float32),
            prompts.astype(jnp.float32),
            rewards,
        ],
        axis=1,
    )
    table = lax.all_gather(local, ("row", "col"), axis=0, tiled=True)
    all_lengths = table[:, 0].astype(jnp.int32)
    all_owners = table[:, 1].astype(jnp.int32)
    all_prompts = table[:, 2].astype(jnp.int32)
    weights = row_weights(all_lengths, all_prompts, table[:, 3], count_prompts)
    offsets = row_offsets(all_lengths, all_owners)
    mine = lax.dynamic_slice_in_dim(weights, lax.axis_index(("row", "col")), 1, 0)
    live = (jnp.arange(slot_count, dtype=jnp.int32) < lengths[0])[:, None]
    upstream = jnp.where(live, roll_cotangent.astype(jnp.float32) * mine[0], 0.0).astype(
        jnp.bfloat16
    )
    hidden_blocks = roll_hidden.reshape(slot_count, col_count, width)
    upstream_blocks = upstream.reshape(slot_count, col_count, width)
    hidden_cols, upstream_cols = (
        lax.all_to_all(hidden_blocks, "col", split_axis=1, concat_axis=1, tiled=True),
        lax.all_to_all(upstream_blocks, "col", split_axis=1, concat_axis=1, tiled=True),
    )
    hidden_all, upstream_all = (
        lax.all_gather(hidden_cols, "row", axis=1, tiled=True),
        lax.all_gather(upstream_cols, "row", axis=1, tiled=True),
    )
    sources = source_index(all_lengths, all_owners, offsets, slot_count, CAPR, total_tokens)
    packed = jnp.take(hidden_all.reshape(-1, width), sources, axis=0, mode="fill", fill_value=0)
    packed_grad = jnp.take(
        upstream_all.reshape(-1, width), sources, axis=0, mode="fill", fill_value=0
    )
    gate_term = jnp.dot(packed, gate_weight, preferred_element_type=jnp.float32)
    up_term = jnp.dot(packed, up_weight, preferred_element_type=jnp.float32)
    gate, upval = (
        lax.psum(gate_term.astype(jnp.bfloat16), "col").astype(jnp.float32),
        lax.psum(up_term.astype(jnp.bfloat16), "col").astype(jnp.float32),
    )
    sig = jax.nn.sigmoid(gate)
    silu = gate * sig
    hidden = (silu * upval).astype(jnp.bfloat16)
    contract_cols = (((1,), (1,)), ((), ()))
    grad_term = lax.dot_general(
        packed_grad, down_weight, contract_cols, preferred_element_type=jnp.float32
    )
    grad_hidden = lax.psum(grad_term.astype(jnp.bfloat16), "col").astype(jnp.float32)
    grad_gate_act = (grad_hidden * upval * sig * (1.0 + gate * (1.0 - sig))).astype(jnp.bfloat16)
    grad_up_act = (grad_hidden * silu).astype(jnp.bfloat16)
    contract_rows = (((0,), (0,)), ((), ()))
    grad_down = lax.dot_general(
        hidden, packed_grad, contract_rows, preferred_element_type=jnp.float32
    ).astype(jnp.bfloat16)
    grad_gate = lax.dot_general(
        packed, grad_gate_act, contract_rows, preferred_element_type=jnp.float32
    ).astype(jnp.bfloat16)
    grad_up = lax.dot_general(
        packed, grad_up_act, contract_rows, preferred_element_type=jnp.float32
    ).astype(jnp.bfloat16)
    term = lax.dot_general(
        grad_gate_act, gate_weight, contract_cols, preferred_element_type=jnp.float32
    )
    grad_input = lax.psum_scatter(
        (
            term
            + lax.dot_general(
                grad_up_act, up_weight, contract_cols, preferred_element_type=jnp.float32
            )
        ).astype(jnp.bfloat16),
        "row",
        scatter_dimension=0,
        tiled=True,
    )
    return (grad_input, grad_gate, grad_up, grad_down)


def solution(mesh):
    return jax.shard_map(
        per_device,
        mesh=mesh,
        in_specs=(
            P(("row", "col"), None),
            P(("row", "col"), None),
            P(("row", "col")),
            P(("row", "col")),
            P(("row", "col")),
            P(("row", "col")),
            P("col", "row"),
            P("col", "row"),
            P("row", "col"),
        ),
        out_specs=(P("row", "col"), P("col", "row"), P("col", "row"), P("row", "col")),
        check_vma=False,
    )
```

profile of v0, /device:TPU:0, one launch (start us, length us, event | category | flops | bytes accessed | tf_op | source)
XLA Modules:
  0.0 450.1 jit_solution(12010402054570381515)
XLA Ops:
  7.2 0.0 all-gather.6.cloned.1.call-start
  7.2 1.2 reshape.123
  8.4 0.1 copy.25
  8.5 12.2 %all_to_all.10 = bf16[42,4,1024]{2,0,1:T(8,128)(2,1)} all-to-all(bf16[42,4,1024]{2,0,1:T(8,128)(2,1)S(1)} %copy.25), channel_id=1, replica_groups=mesh['row'=8,'col'=4] {'col'}, dimensions={1} | all-to-all | bytes 688128 | tf_op jit(solution)/shard_map/all_to_all | solution.py:79
  20.7 0.0 all-gather.6.cloned.1.call-update
  20.8 0.0 all-gather.4.cloned.1.call-start
  23.4 0.1 maximum_bitcast_fusion
  23.5 66.8 %all-gather = f32[32,1,4]{2,1,0:T(1,128)S(1)} all-gather(f32[1,1,4]{2,1,0:T(1,128)S(1)} %maximum_bitcast_fusion), channel_id=1, replica_groups=mesh['row'=8,'col'=4] {'row','col'}, dimensions={0}, use_global_device_ids=true | all-gather | bytes 528 | tf_op jit(solution)/shard_map/all_gather | solution.py:65
  90.2 0.1 copy.22
  90.3 0.2 convert_reduce_fusion
  90.5 0.1 select_reduce_fusion.3
  90.6 0.1 select_reduce_fusion.2
  90.7 0.1 select_reduce_fusion.1
  90.8 0.6 dynamic_slice.3
  91.4 1.8 select_convert_fusion
  93.2 0.2 reshape.121
  93.4 0.1 copy.23
  93.5 9.5 %all_to_all.11 = bf16[42,4,1024]{2,0,1:T(8,128)(2,1)} all-to-all(bf16[42,4,1024]{2,0,1:T(8,128)(2,1)S(1)} %copy.23), channel_id=1, replica_groups=mesh['row'=8,'col'=4] {'col'}, dimensions={1} | all-to-all | bytes 688128 | tf_op jit(solution)/shard_map/all_to_all | solution.py:80
  103.0 0.0 all-gather.4.cloned.1.call-update
  103.0 0.0 all-reduce.3.cloned.1.call-start
  103.1 0.1 reshape.145
  103.2 0.2 select_reduce_fusion
  103.4 0.1 add_select_fusion
  103.5 0.1 select_n.47
  103.6 7.6 %scatter_custom_fusion = s32[1024]{0:T(1024)S(1)} fusion(s32[1344]{0:T(1024)S(1)} %fusion.15, s32[1344]{0:T(1024)S(1)} %reshape.145, s32[]{:T(128)} %constant.14.clone.1), kind=kCustom, calls=%fused_computation.40 | custom fusion | bytes 4100 | tf_op jit(solution)/shard_map/scatter | solution.py:36
  111.3 0.0 all-gather.6.cloned.1.call-done
  111.3 3.4 copy.26
  114.7 5.5 %gather_fusion.1 = bf16[1024,1024]{1,0:T(8,128)(2,1)} fusion(bf16[1344,1024]{1,0:T(8,128)(2,1)S(1)} %bitcast.48, s32[1024]{0:T(1024)S(1)} %fusion.16), kind=kCustom, calls=%fused_computation.1.clone | custom fusion | bytes 4198400 | tf_op jit(solution)/shard_map/jit(_take)/gather | solution.py:87
  120.2 17.9 %all-gather.4.cloned.1.call-done = bf16[42,32,1024]{2,0,1:T(8,128)(2,1)} async-done(((bf16[42,4,1024]{2,0,1:T(8,128)(2,1)}), bf16[42,32,1024]{2,0,1:T(8,128)(2,1)}) %all-gather.4.cloned.1.call-update) | async-done | bytes 2752528 | tf_op jit(solution)/shard_map/all_gather | solution.py:84
  138.1 3.4 copy.24
  141.5 5.4 %gather_fusion = bf16[1024,1024]{1,0:T(8,128)(2,1)} fusion(bf16[1344,1024]{1,0:T(8,128)(2,1)S(1)} %bitcast.47, s32[1024]{0:T(1024)S(1)} %fusion.16), kind=kCustom, calls=%fused_computation.clone | custom fusion | bytes 4198400 | tf_op jit(solution)/shard_map/jit(_take)/gather | solution.py:88
  146.8 8.9 %convolution_convert_fusion.2 = bf16[1024,1848]{0,1:T(8,128)(2,1)} fusion(bf16[1024,1848]{0,1:T(8,128)(2,1)} %param.17, bf16[1024,1024]{1,0:T(8,128)(2,1)} %gather_fusion.1, pred[1024]{0:T(1024)(128)(4,1)S(1)} %compare_and_fusion), kind=kOutput, calls=%fused_computation.23 | convolution fusion | flops 3878477824 | bytes 9667584 | tf_op jit(solution)/shard_map/dot_general | solution.py:91
  155.8 0.0 copy-start.9
  155.8 6.3 %convolution_convert_fusion.3 = bf16[1024,1848]{0,1:T(8,128)(2,1)} fusion(bf16[1024,1848]{0,1:T(8,128)(2,1)S(1)} %copy-done.11, bf16[1024,1024]{1,0:T(8,128)(2,1)S(1)} %copy-done.6, pred[1024]{0:T(1024)(128)(4,1)S(1)} %compare_and_fusion), kind=kOutput, calls=%fused_computation.24 | convolution fusion | flops 3878477824 | bytes 9667584 | tf_op jit(solution)/shard_map/dot_general | solution.py:92
  162.2 6.3 %convolution_convert_fusion.4 = bf16[1024,1848]{0,1:T(8,128)(2,1)} fusion(bf16[1848,1024]{1,0:T(8,128)(2,1)S(1)} %copy-done.9, bf16[1024,1024]{1,0:T(8,128)(2,1)S(1)} %copy-done.7, pred[1024]{0:T(1024)(128)(4,1)S(1)} %compare_and_fusion), kind=kOutput, calls=%fused_computation.25 | convolution fusion | flops 3878477824 | bytes 9667584 | tf_op jit(solution)/shard_map/dot_general | solution.py:101
  168.5 0.0 all-reduce.3.cloned.1.call-update
  168.5 0.0 reduce-scatter.2.cloned.1.call-start
  168.6 219.0 %all-reduce.3.cloned.1.call-done = (bf16[1024,1848]{0,1:T(8,128)(2,1)}, bf16[1024,1848]{0,1:T(8,128)(2,1)}, bf16[1024,1848]{0,1:T(8,128)(2,1)}) async-done(((bf16[1024,1848]{0,1:T(8,128)(2,1)}, bf16[1024,1848]{0,1:T(8,128)(2,1)}, bf16[1024,1848]{0,1:T(8,128)(2,1)}), (bf16[1024,1848]{0,1:T(8,128)(2,1)}, bf16[1024,1848]{0,1:T(8,128)(2,1)}, bf16[1024,1848]{0,1:T(8,128)(2,1)})) %all-reduce.3.cloned.1.call-update) | async-done | bytes 11354128 | tf_op jit(solution)/shard_map/psum | solution.py:95
  387.5 6.3 %fusion.3 = bf16[1024,1848]{0,1:T(8,128)(2,1)S(1)} fusion(bf16[1024,1848]{0,1:T(8,128)(2,1)} %get-tuple-element.7, bf16[1024,1848]{0,1:T(8,128)(2,1)} %get-tuple-element.8, bf16[1024,1848]{0,1:T(8,128)(2,1)} %get-tuple-element.9), kind=kLoop, calls=%fused_computation.12 | loop fusion | flops 24600576 | bytes 15138816 | tf_op jit(solution)/shard_map/convert_element_type | solution.py:105
  393.8 0.0 copy-start.5
  393.8 1.9 copy-done.5
  395.7 4.7 %fusion.27 = f32[1024,1024]{1,0:T(8,128)S(1)} fusion(bf16[1024,1848]{0,1:T(8,128)(2,1)S(1)} %fusion.3, bf16[1024,1848]{0,1:T(8,128)(2,1)S(1)} %copy-done.10), kind=kOutput, calls=%fused_computation.66 | convolution fusion | flops 3875536896 | bytes 11763712 | tf_op jit(solution)/shard_map/dot_general | solution.py:117
  400.5 6.3 %add_convert_fusion = bf16[1024,1024]{1,0:T(8,128)(2,1)} fusion(f32[1024,1024]{1,0:T(8,128)S(1)} %fusion.27, bf16[1024,1848]{0,1:T(8,128)(2,1)S(1)} %copy-done.12, bf16[1024,1848]{0,1:T(8,128)(2,1)S(1)} %copy-done.3, bf16[1024,1848]{0,1:T(8,128)(2,1)S(1)} %copy-done.1), kind=kOutput, calls=%fused_computation.18 | convolution fusion | flops 3892772864 | bytes 17645568 | tf_op jit(solution)/shard_map/dot_general | solution.py:123
  406.8 0.0 reduce-scatter.2.cloned.1.call-update
  406.8 7.9 %convolution_convert_fusion.1 = bf16[1024,1848]{0,1:T(8,128)(2,1)} fusion(bf16[1024,1848]{0,1:T(8,128)(2,1)} %copy-done.5, bf16[1024,1024]{1,0:T(8,128)(2,1)S(1)} %copy-done.6, pred[1024]{0:T(1024)(128)(4,1)S(1)} %compare_and_fusion), kind=kOutput, calls=%fused_computation.22 | convolution fusion | flops 3878477824 | bytes 9667584 | tf_op jit(solution)/shard_map/dot_general | solution.py:111
  414.7 6.4 %convolution_convert_fusion = bf16[1024,1848]{0,1:T(8,128)(2,1)} fusion(bf16[1024,1024]{1,0:T(8,128)(2,1)S(1)} %copy-done.6, pred[1024]{0:T(1024)(128)(4,1)S(1)} %compare_and_fusion, bf16[1024,1848]{0,1:T(8,128)(2,1)S(1)} %copy-done.4, bf16[1024,1848]{0,1:T(8,128)(2,1)S(1)} %copy-done.2), kind=kOutput, calls=%fused_computation.21 | convolution fusion | flops 3893616640 | bytes 13452288 | tf_op jit(solution)/shard_map/dot_general | solution.py:114
  421.2 6.4 %fusion.11 = bf16[1848,1024]{1,0:T(8,128)(2,1)} fusion(bf16[1024,1848]{0,1:T(8,128)(2,1)S(1)} %copy-done, bf16[1024,1848]{0,1:T(8,128)(2,1)S(1)} %copy-done.2, bf16[1024,1024]{1,0:T(8,128)(2,1)S(1)} %copy-done.8, pred[1024]{0:T(1024)(128)(4,1)S(1)} %compare_and_fusion), kind=kOutput, calls=%fused_computation.20 | convolution fusion | flops 3893616640 | bytes 13452288 | tf_op jit(solution)/shard_map/dot_general | solution.py:108
  427.6 16.0 %reduce-scatter.2.cloned.1.call-done = bf16[128,1024]{1,0:T(8,128)(2,1)} async-done(((bf16[1024,1024]{1,0:T(8,128)(2,1)}), bf16[128,1024]{1,0:T(8,128)(2,1)}) %reduce-scatter.2.cloned.1.call-update) | async-done | bytes 262160 | tf_op jit(solution)/shard_map/reduce_scatter | solution.py:120
  (35 shorter events, 0.2 us)
Async XLA Ops:
  7.2 104.1 %all-gather.6.cloned.1.call-start = ((), (), s32[]{:S(2)}) async-start(), calls=%async_computation.4 | async-start | bytes 3538944 | tf_op jit(solution)/shard_map/all_gather | solution.py:83
  20.8 117.3 %all-gather.4.cloned.1.call-start = ((), (), s32[]{:S(2)}) async-start(), calls=%async_computation.3 | async-start | bytes 3538944 | tf_op jit(solution)/shard_map/all_gather | solution.py:84
  103.0 284.5 %all-reduce.3.cloned.1.call-start = ((), (), s32[]{:S(2)}) async-start(), calls=%async_computation.6 | async-start | bytes 22708224 | tf_op jit(solution)/shard_map/psum | solution.py:95
  146.8 9.0 %copy-start.6 = (bf16[1024,1024]{1,0:T(8,128)(2,1)S(1)}, bf16[1024,1024]{1,0:T(8,128)(2,1)}, u32[]{:S(2)}) copy-start(bf16[1024,1024]{1,0:T(8,128)(2,1)} %gather_fusion.1) | copy-start | bytes 6291460
  146.8 9.0 %copy-start.11 = (bf16[1024,1848]{0,1:T(8,128)(2,1)S(1)}, bf16[1024,1848]{0,1:T(8,128)(2,1)}, u32[]{:S(2)}) copy-start(bf16[1024,1848]{0,1:T(8,128)(2,1)} %param.18) | copy-start | bytes 11354116
  155.8 6.4 %copy-start.7 = (bf16[1024,1024]{1,0:T(8,128)(2,1)S(1)}, bf16[1024,1024]{1,0:T(8,128)(2,1)}, u32[]{:S(2)}) copy-start(bf16[1024,1024]{1,0:T(8,128)(2,1)} %gather_fusion) | copy-start | bytes 6291460
  155.8 6.4 %copy-start.9 = (bf16[1848,1024]{1,0:T(8,128)(2,1)S(1)}, bf16[1848,1024]{1,0:T(8,128)(2,1)}, u32[]{:S(2)}) copy-start(bf16[1848,1024]{1,0:T(8,128)(2,1)} %param.19) | copy-start | bytes 11354116
  168.5 275.0 %reduce-scatter.2.cloned.1.call-start = ((), (), s32[]{:S(2)}) async-start(), calls=%async_computation.5 | async-start | bytes 2359296 | tf_op jit(solution)/shard_map/reduce_scatter | solution.py:120
  387.5 8.2 %copy-start.10 = (bf16[1024,1848]{0,1:T(8,128)(2,1)S(1)}, bf16[1024,1848]{0,1:T(8,128)(2,1)}, u32[]{:S(2)}) copy-start(bf16[1024,1848]{0,1:T(8,128)(2,1)} %param.17) | copy-start | bytes 11354116
  393.8 1.9 copy-start.5
  395.7 4.8 %copy-start.1 = (bf16[1024,1848]{0,1:T(8,128)(2,1)S(1)}, bf16[1024,1848]{0,1:T(8,128)(2,1)}, u32[]{:S(2)}) copy-start(bf16[1024,1848]{0,1:T(8,128)(2,1)} %get-tuple-element.9) | copy-start | bytes 11354116
  395.7 4.8 %copy-start.3 = (bf16[1024,1848]{0,1:T(8,128)(2,1)S(1)}, bf16[1024,1848]{0,1:T(8,128)(2,1)}, u32[]{:S(2)}) copy-start(bf16[1024,1848]{0,1:T(8,128)(2,1)} %get-tuple-element.8) | copy-start | bytes 11354116
  395.7 4.8 %copy-start.12 = (bf16[1024,1848]{0,1:T(8,128)(2,1)S(1)}, bf16[1024,1848]{0,1:T(8,128)(2,1)}, u32[]{:S(2)}) copy-start(bf16[1024,1848]{0,1:T(8,128)(2,1)} %param.18) | copy-start | bytes 11354116
  406.8 7.9 %copy-start.2 = (bf16[1024,1848]{0,1:T(8,128)(2,1)S(1)}, bf16[1024,1848]{0,1:T(8,128)(2,1)}, u32[]{:S(2)}) copy-start(bf16[1024,1848]{0,1:T(8,128)(2,1)} %get-tuple-element.9) | copy-start | bytes 11354116
  406.8 7.9 %copy-start.4 = (bf16[1024,1848]{0,1:T(8,128)(2,1)S(1)}, bf16[1024,1848]{0,1:T(8,128)(2,1)}, u32[]{:S(2)}) copy-start(bf16[1024,1848]{0,1:T(8,128)(2,1)} %get-tuple-element.8) | copy-start | bytes 11354116
  414.7 6.4 %copy-start = (bf16[1024,1848]{0,1:T(8,128)(2,1)S(1)}, bf16[1024,1848]{0,1:T(8,128)(2,1)}, u32[]{:S(2)}) copy-start(bf16[1024,1848]{0,1:T(8,128)(2,1)} %get-tuple-element.7) | copy-start | bytes 11354116
  414.7 6.4 %copy-start.8 = (bf16[1024,1024]{1,0:T(8,128)(2,1)S(1)}, bf16[1024,1024]{1,0:T(8,128)(2,1)}, u32[]{:S(2)}) copy-start(bf16[1024,1024]{1,0:T(8,128)(2,1)} %gather_fusion) | copy-start | bytes 6291460
Sparse Core Ops, SparseCore 0:
  20.9 37.9 all-gather.5
  103.1 34.8 all-gather.3
  168.6 218.8 all-reduce.2
  406.9 36.5 reduce-scatter.1
where the time goes:
time: 450 us
  waiting for transfers between devices  253 us (56%)
  blocking collectives  88.5 us (20%)
  matrix products  53.4 us (12%)
  local copies, waits for them, and re-layouts  29.7 us (7%)
  between operations  16.6 us (4%)
  other arithmetic  8.91 us (2%)
    psum x1, waiting for transfers between devices, per_device(): lax.psum(up_term.astype(jnp.bfloat16), 'col').astype(jnp.float32)  219 us
    all_gather x1, blocking collectives, per_device(): table = lax.all_gather(local, ('row', 'col'), axis=0, tiled=True)  66.8 us
    all_gather x1, waiting for transfers between devices, per_device(): lax.all_gather(upstream_cols, 'row', axis=1, tiled=True)  17.9 us
    reduce_scatter x1, waiting for transfers between devices, per_device(): lax.psum_scatter((term + lax.dot_general(grad_up_act, up_weight, contract...  16 us
    all_to_all x1, blocking collectives, per_device(): lax.all_to_all(hidden_blocks, 'col', split_axis=1, concat_axis=1, tiled=T...  12.2 us
    all_to_all x1, blocking collectives, per_device(): lax.all_to_all(upstream_blocks, 'col', split_axis=1, concat_axis=1, tiled...  9.51 us
  transfers between devices with their start and end apart: 4, of which 3 were waited for; matrix products, arithmetic and copies ran while one was open for 9% of the time, Pallas kernels for 0%

commit v1 on v0

--- a/solution.py
+++ b/solution.py
@@ -92,7 +92,7 @@
     up_term = jnp.dot(packed, up_weight, preferred_element_type=jnp.float32)
     gate, upval = (
         lax.psum(gate_term.astype(jnp.bfloat16), "col").astype(jnp.float32),
-        lax.psum(up_term.astype(jnp.bfloat16), "col").astype(jnp.float32),
+        jnp.sum(lax.all_gather(up_term.astype(jnp.bfloat16), "col"), axis=0).astype(jnp.float32),
     )
     sig = jax.nn.sigmoid(gate)
     silu = gate * sig

time: 450 us -> 517 us (1.15); the launches traced: 450 us -> 509 us
  local copies, waits for them, and re-layouts: 29.7 us -> 61.3 us
  other arithmetic: 8.91 us -> 30.8 us
  matrix products: 53.4 us -> 58.8 us
    all_gather x0 -> x1, waiting for transfers between devices: none -> 120 us  [per_device(): lax.all_gather(up_term.astype(jnp.bfloat16), 'col')]
    psum x1, waiting for transfers between devices: 219 us -> 110 us  [per_device(): lax.psum(grad_term.astype(jnp.bfloat16), 'col').astype(jnp.float32)]
    all_gather x0 -> x1, local copies, waits for them, and re-layouts: none -> 31.8 us  [per_device(): lax.all_gather(up_term.astype(jnp.bfloat16), 'col')]
    reduce_sum x0 -> x1, other arithmetic: none -> 21.9 us  [per_device(): jnp.sum(lax.all_gather(up_term.astype(jnp.bfloat16), 'col'), axis=0)]
    all_gather x1, waiting for transfers between devices: 17.9 us -> 8.62 us  [per_device(): lax.all_gather(upstream_cols, 'row', axis=1, tiled=True)]
  transfers between devices with their start and end apart: 4 -> 5, of which waited for: 3 -> 4; matrix products, arithmetic and copies ran while one was open for 9% -> 26% of each run, Pallas kernels for 0% -> 0%
where the time goes in v1:
time: 517 us; the launch traced here: 509 us
  waiting for transfers between devices  252 us (49%)
  blocking collectives  88.5 us (17%)
  local copies, waits for them, and re-layouts  61.3 us (12%)
  matrix products  58.8 us (11%)
  other arithmetic  30.8 us (6%)
  between operations  16.8 us (3%)
    all_gather x1, waiting for transfers between devices, per_device(): lax.all_gather(up_term.astype(jnp.bfloat16), 'col')  120 us
    psum x1, waiting for transfers between devices, per_device(): lax.psum(grad_term.astype(jnp.bfloat16), 'col').astype(jnp.float32)  110 us
    all_gather x1, blocking collectives, per_device(): table = lax.all_gather(local, ('row', 'col'), axis=0, tiled=True)  66.8 us
    all_gather x1, local copies, waits for them, and re-layouts, per_device(): lax.all_gather(up_term.astype(jnp.bfloat16), 'col')  31.8 us
    reduce_sum x1, other arithmetic, per_device(): jnp.sum(lax.all_gather(up_term.astype(jnp.bfloat16), 'col'), axis=0)  21.9 us
    reduce_scatter x1, waiting for transfers between devices, per_device(): lax.psum_scatter((term + lax.dot_general(grad_up_act, up_weight, contract...  14.5 us
    all_to_all x1, blocking collectives, per_device(): lax.all_to_all(hidden_blocks, 'col', split_axis=1, concat_axis=1, tiled=T...  12.2 us
  transfers between devices with their start and end apart: 5, of which 4 were waited for; matrix products, arithmetic and copies ran while one was open for 26% of the time, Pallas kernels for 0%

profile of v1, /device:TPU:0, one launch (start us, length us, event | category | flops | bytes accessed | tf_op | source)
XLA Modules:
  0.0 509.4 jit_solution(11023067013493813053)
XLA Ops:
  7.2 0.0 all-gather.8.cloned.1.call-start
  7.2 1.2 reshape.123
  8.4 0.1 copy.25
  8.5 12.2 %all_to_all.10 = bf16[42,4,1024]{2,0,1:T(8,128)(2,1)} all-to-all(bf16[42,4,1024]{2,0,1:T(8,128)(2,1)S(1)} %copy.25), channel_id=1, replica_groups=mesh['row'=8,'col'=4] {'col'}, dimensions={1} | all-to-all | bytes 688128 | tf_op jit(solution)/shard_map/all_to_all | solution.py:79
  20.7 0.0 all-gather.8.cloned.1.call-update
  20.8 0.0 all-gather.6.cloned.1.call-start
  23.4 0.1 maximum_bitcast_fusion
  23.5 66.8 %all-gather.1 = f32[32,1,4]{2,1,0:T(1,128)S(1)} all-gather(f32[1,1,4]{2,1,0:T(1,128)S(1)} %maximum_bitcast_fusion), channel_id=1, replica_groups=mesh['row'=8,'col'=4] {'row','col'}, dimensions={0}, use_global_device_ids=true | all-gather | bytes 528 | tf_op jit(solution)/shard_map/all_gather | solution.py:65
  90.2 0.1 copy.22
  90.3 0.1 convert_reduce_fusion
  90.5 0.1 select_reduce_fusion.3
  90.6 0.1 select_reduce_fusion.2
  90.7 0.1 select_reduce_fusion.1
  90.8 0.6 dynamic_slice.3
  91.4 1.8 select_convert_fusion
  93.2 0.2 reshape.121
  93.4 0.1 copy.23
  93.5 9.5 %all_to_all.11 = bf16[42,4,1024]{2,0,1:T(8,128)(2,1)} all-to-all(bf16[42,4,1024]{2,0,1:T(8,128)(2,1)S(1)} %copy.23), channel_id=1, replica_groups=mesh['row'=8,'col'=4] {'col'}, dimensions={1} | all-to-all | bytes 688128 | tf_op jit(solution)/shard_map/all_to_all | solution.py:80
  103.0 0.0 all-gather.6.cloned.1.call-update
  103.0 0.0 all-gather.10.cloned.1.call-start
  103.1 0.2 select_reduce_fusion
  103.3 0.1 add_select_fusion
  103.3 0.1 select_n.47
  103.5 0.1 reshape.145
  103.6 7.6 %scatter_custom_fusion = s32[1024]{0:T(1024)S(1)} fusion(s32[1344]{0:T(1024)S(1)} %fusion.15, s32[1344]{0:T(1024)S(1)} %reshape.145, s32[]{:T(128)} %constant.20.clone.1), kind=kCustom, calls=%fused_computation.40 | custom fusion | bytes 4100 | tf_op jit(solution)/shard_map/scatter | solution.py:36
  111.3 0.0 all-gather.8.cloned.1.call-done
  111.3 3.4 copy.26
  114.7 5.3 %gather_fusion.1 = bf16[1024,1024]{1,0:T(8,128)(2,1)} fusion(bf16[1344,1024]{1,0:T(8,128)(2,1)S(1)} %bitcast.49, s32[1024]{0:T(1024)S(1)} %fusion.16), kind=kCustom, calls=%fused_computation.1.clone | custom fusion | bytes 4198400 | tf_op jit(solution)/shard_map/jit(_take)/gather | solution.py:87
  120.0 8.9 %convolution_convert_fusion.3 = bf16[1024,1848]{0,1:T(8,128)(2,1)} fusion(bf16[1024,1848]{0,1:T(8,128)(2,1)} %param.18, bf16[1024,1024]{1,0:T(8,128)(2,1)} %gather_fusion.1, pred[1024]{0:T(1024)(128)(4,1)S(1)} %compare_and_fusion), kind=kOutput, calls=%fused_computation.24 | convolution fusion | flops 3878477824 | bytes 9667584 | tf_op jit(solution)/shard_map/dot_general | solution.py:92
  128.9 0.5 all-reduce.3.cloned.1.call-start
  129.5 8.6 %all-gather.6.cloned.1.call-done = bf16[42,32,1024]{2,0,1:T(8,128)(2,1)} async-done(((bf16[42,4,1024]{2,0,1:T(8,128)(2,1)}), bf16[42,32,1024]{2,0,1:T(8,128)(2,1)}) %all-gather.6.cloned.1.call-update) | async-done | bytes 2752528 | tf_op jit(solution)/shard_map/all_gather | solution.py:84
  138.1 3.4 copy.24
  141.5 5.4 %gather_fusion = bf16[1024,1024]{1,0:T(8,128)(2,1)} fusion(bf16[1344,1024]{1,0:T(8,128)(2,1)S(1)} %bitcast.48, s32[1024]{0:T(1024)S(1)} %fusion.16), kind=kCustom, calls=%fused_computation.clone | custom fusion | bytes 4198400 | tf_op jit(solution)/shard_map/jit(_take)/gather | solution.py:88
  146.8 10.2 %convolution_convert_fusion.2 = bf16[1024,1848]{0,1:T(8,128)(2,1)} fusion(bf16[1024,1848]{0,1:T(8,128)(2,1)} %param.17, bf16[1024,1024]{1,0:T(8,128)(2,1)} %gather_fusion.1, pred[1024]{0:T(1024)(128)(4,1)S(1)} %compare_and_fusion), kind=kOutput, calls=%fused_computation.23 | convolution fusion | flops 3878477824 | bytes 9667584 | tf_op jit(solution)/shard_map/dot_general | solution.py:91
  157.0 6.3 %convolution_convert_fusion.4 = bf16[1024,1848]{0,1:T(8,128)(2,1)} fusion(bf16[1848,1024]{1,0:T(8,128)(2,1)S(1)} %copy-done.9, bf16[1024,1024]{1,0:T(8,128)(2,1)S(1)} %copy-done.7, pred[1024]{0:T(1024)(128)(4,1)S(1)} %compare_and_fusion), kind=kOutput, calls=%fused_computation.25 | convolution fusion | flops 3878477824 | bytes 9667584 | tf_op jit(solution)/shard_map/dot_general | solution.py:101
  163.4 0.2 reduce-scatter.2.cloned.1.call-start
  163.6 119.5 %all-gather.10.cloned.1.call-done = bf16[4096,1848]{0,1:T(8,128)(2,1)} async-done(((bf16[1024,1848]{0,1:T(8,128)(2,1)}), bf16[4096,1848]{0,1:T(8,128)(2,1)}) %all-gather.10.cloned.1.call-update) | async-done | bytes 15138832 | tf_op jit(solution)/shard_map/all_gather | solution.py:95
  283.1 31.8 %reshape.149 = bf16[4,1024,1848]{1,0,2:T(4,128)(2,1)} reshape(bf16[4096,1848]{0,1:T(8,128)(2,1)} %all-gather.10.cloned.1.call-done) | data formatting | bytes 30277632 | tf_op jit(solution)/shard_map/all_gather | solution.py:95
  314.9 21.9 %reduce_sum.78 = bf16[1024,1848]{0,1:T(8,128)(2,1)} reduce(bf16[4,1024,1848]{1,0,2:T(4,128)(2,1)} %reshape.149, bf16[]{:T(256)} %constant.46.clone.1), dimensions={0}, to_apply=%region_8.10 | reduce | flops 5677056 | bytes 18923522 | tf_op jit(solution)/shard_map/reduce_sum | solution.py:95
  336.7 109.8 %all-reduce.3.cloned.1.call-done = (bf16[1024,1848]{0,1:T(8,128)(2,1)}, bf16[1024,1848]{0,1:T(8,128)(2,1)}) async-done(((bf16[1024,1848]{0,1:T(8,128)(2,1)}, bf16[1024,1848]{0,1:T(8,128)(2,1)}), (bf16[1024,1848]{0,1:T(8,128)(2,1)}, bf16[1024,1848]{0,1:T(8,128)(2,1)})) %all-reduce.3.cloned.1.call-update) | async-done | bytes 7569424 | tf_op jit(solution)/shard_map/psum | solution.py:104
  446.5 6.3 %fusion.3 = bf16[1024,1848]{0,1:T(8,128)(2,1)S(1)} fusion(bf16[1024,1848]{0,1:T(8,128)(2,1)} %reduce_sum.78, bf16[1024,1848]{0,1:T(8,128)(2,1)} %get-tuple-element.7, bf16[1024,1848]{0,1:T(8,128)(2,1)} %get-tuple-element.8), kind=kLoop, calls=%fused_computation.12 | loop fusion | flops 24600576 | bytes 15138816 | tf_op jit(solution)/shard_map/convert_element_type | solution.py:105
  452.8 1.9 copy-done.4
  454.7 4.7 fusion.27
  459.5 6.6 %add_convert_fusion = bf16[1024,1024]{1,0:T(8,128)(2,1)} fusion(f32[1024,1024]{1,0:T(8,128)S(1)} %fusion.27, bf16[1024,1848]{0,1:T(8,128)(2,1)S(1)} %copy-done.11, bf16[1024,1848]{0,1:T(8,128)(2,1)S(1)} %copy-done.3, bf16[1024,1848]{0,1:T(8,128)(2,1)S(1)} %copy-done.1), kind=kOutput, calls=%fused_computation.18 | convolution fusion | flops 3892772864 | bytes 17645568 | tf_op jit(solution)/shard_map/dot_general | solution.py:123
  466.1 9.9 %convolution_convert_fusion = bf16[1024,1848]{0,1:T(8,128)(2,1)} fusion(bf16[1024,1024]{1,0:T(8,128)(2,1)S(1)} %copy-done.6, pred[1024]{0:T(1024)(128)(4,1)S(1)} %compare_and_fusion, bf16[1024,1848]{0,1:T(8,128)(2,1)} %get-tuple-element.7, bf16[1024,1848]{0,1:T(8,128)(2,1)} %get-tuple-element.8), kind=kOutput, calls=%fused_computation.21 | convolution fusion | flops 3893616640 | bytes 13452288 | tf_op jit(solution)/shard_map/dot_general | solution.py:114
  476.0 5.7 %convolution_convert_fusion.1 = bf16[1024,1848]{0,1:T(8,128)(2,1)} fusion(bf16[1024,1848]{0,1:T(8,128)(2,1)S(1)} %copy-done.5, bf16[1024,1024]{1,0:T(8,128)(2,1)S(1)} %copy-done.6, pred[1024]{0:T(1024)(128)(4,1)S(1)} %compare_and_fusion), kind=kOutput, calls=%fused_computation.22 | convolution fusion | flops 3878477824 | bytes 9667584 | tf_op jit(solution)/shard_map/dot_general | solution.py:111
  481.7 6.4 %fusion.11 = bf16[1848,1024]{1,0:T(8,128)(2,1)} fusion(bf16[1024,1848]{0,1:T(8,128)(2,1)S(1)} %copy-done, bf16[1024,1848]{0,1:T(8,128)(2,1)S(1)} %copy-done.2, bf16[1024,1024]{1,0:T(8,128)(2,1)S(1)} %copy-done.8, pred[1024]{0:T(1024)(128)(4,1)S(1)} %compare_and_fusion), kind=kOutput, calls=%fused_computation.20 | convolution fusion | flops 3893616640 | bytes 13452288 | tf_op jit(solution)/shard_map/dot_general | solution.py:108
  488.2 14.5 %reduce-scatter.2.cloned.1.call-done = bf16[128,1024]{1,0:T(8,128)(2,1)} async-done(((bf16[1024,1024]{1,0:T(8,128)(2,1)}), bf16[128,1024]{1,0:T(8,128)(2,1)}) %reduce-scatter.2.cloned.1.call-update) | async-done | bytes 262160 | tf_op jit(solution)/shard_map/reduce_scatter | solution.py:120
  (38 shorter events, 0.2 us)
Async XLA Ops:
  7.2 104.1 %all-gather.8.cloned.1.call-start = ((), (), s32[]{:S(2)}) async-start(), calls=%async_computation.4 | async-start | bytes 3538944 | tf_op jit(solution)/shard_map/all_gather | solution.py:83
  20.8 117.3 %all-gather.6.cloned.1.call-start = ((), (), s32[]{:S(2)}) async-start(), calls=%async_computation.3 | async-start | bytes 3538944 | tf_op jit(solution)/shard_map/all_gather | solution.py:84
  103.0 180.1 %all-gather.10.cloned.1.call-start = ((), (), s32[]{:S(2)}) async-start(), calls=%async_computation.6 | async-start | bytes 18923520 | tf_op jit(solution)/shard_map/all_gather | solution.py:95
  128.9 317.6 %all-reduce.3.cloned.1.call-start = ((), (), s32[]{:S(2)}) async-start(), calls=%async_computation.7 | async-start | bytes 15138816 | tf_op jit(solution)/shard_map/psum | solution.py:104
  146.8 10.2 %copy-start.7 = (bf16[1024,1024]{1,0:T(8,128)(2,1)S(1)}, bf16[1024,1024]{1,0:T(8,128)(2,1)}, u32[]{:S(2)}) copy-start(bf16[1024,1024]{1,0:T(8,128)(2,1)} %gather_fusion) | copy-start | bytes 6291460
  146.8 10.2 %copy-start.9 = (bf16[1848,1024]{1,0:T(8,128)(2,1)S(1)}, bf16[1848,1024]{1,0:T(8,128)(2,1)}, u32[]{:S(2)}) copy-start(bf16[1848,1024]{1,0:T(8,128)(2,1)} %param.19) | copy-start | bytes 11354116
  163.4 339.3 %reduce-scatter.2.cloned.1.call-start = ((), (), s32[]{:S(2)}) async-start(), calls=%async_computation.5 | async-start | bytes 2359296 | tf_op jit(solution)/shard_map/reduce_scatter | solution.py:120
  446.5 8.2 %copy-start.10 = (bf16[1024,1848]{0,1:T(8,128)(2,1)S(1)}, bf16[1024,1848]{0,1:T(8,128)(2,1)}, u32[]{:S(2)}) copy-start(bf16[1024,1848]{0,1:T(8,128)(2,1)} %param.17) | copy-start | bytes 11354116
  452.8 1.9 copy-start.4
  454.7 4.8 copy-start.1
  454.7 4.8 copy-start.3
  454.7 4.8 copy-start.11
  459.5 6.6 %copy-start.6 = (bf16[1024,1024]{1,0:T(8,128)(2,1)S(1)}, bf16[1024,1024]{1,0:T(8,128)(2,1)}, u32[]{:S(2)}) copy-start(bf16[1024,1024]{1,0:T(8,128)(2,1)} %gather_fusion.1) | copy-start | bytes 6291460
  466.1 9.9 %copy-start.5 = (bf16[1024,1848]{0,1:T(8,128)(2,1)S(1)}, bf16[1024,1848]{0,1:T(8,128)(2,1)}, u32[]{:S(2)}) copy-start(bf16[1024,1848]{0,1:T(8,128)(2,1)} %copy-done.4) | copy-start | bytes 11354116
  476.0 5.7 %copy-start = (bf16[1024,1848]{0,1:T(8,128)(2,1)S(1)}, bf16[1024,1848]{0,1:T(8,128)(2,1)}, u32[]{:S(2)}) copy-start(bf16[1024,1848]{0,1:T(8,128)(2,1)} %reduce_sum.78) | copy-start | bytes 11354116
  476.0 5.7 %copy-start.2 = (bf16[1024,1848]{0,1:T(8,128)(2,1)S(1)}, bf16[1024,1848]{0,1:T(8,128)(2,1)}, u32[]{:S(2)}) copy-start(bf16[1024,1848]{0,1:T(8,128)(2,1)} %get-tuple-element.8) | copy-start | bytes 11354116
  476.0 5.7 %copy-start.8 = (bf16[1024,1024]{1,0:T(8,128)(2,1)S(1)}, bf16[1024,1024]{1,0:T(8,128)(2,1)}, u32[]{:S(2)}) copy-start(bf16[1024,1024]{1,0:T(8,128)(2,1)} %gather_fusion) | copy-start | bytes 6291460
Sparse Core Ops, SparseCore 0:
  20.9 37.9 all-gather.7
  103.1 34.8 all-gather.5
  140.5 142.5 all-gather.9
  287.1 159.3 all-reduce.2
  466.2 36.4 reduce-scatter.1
